TPU v7x, 32 devices: a whole 2x2x4 slice. The times are simulated.
32 devices in a mesh: prow: 8 (over z, core), pcol: 4 (over y, x).
Axes of the slice: x: 2, y: 2, z: 4, core: 2. Of those that a mesh axis runs over, the one named last changes fastest.
Arguments:
- tri_corners: float32 [9, 2048], P(None, ('prow', 'pcol')), may hold values from -1.6 to 1.6, as said below
- edge_tris: int32 [2, 2048], P(None, 'prow'), may hold values from 0 to 2047, as said below
- edge_free: int32 [2, 2048], P(None, 'prow'), may hold values from 0 to 2
- pivots: int32 [1, 256], replicated, may hold values from 0 to 2047, as said below
- lower_inv: float32 [1, 2, 256, 256], P(None, None, 'prow'), may hold values from -1 to 1, as said below
- upper_inv: float32 [1, 2, 256, 256], P(None, None, 'prow'), may hold values from -2 to 2, as said below
Outputs:
- slab_matrix: float32 [2048, 1024], P('prow', 'pcol')
Inputs may be any that keep to these rules, and one draw needn't show every extreme that they name: `tri_corners`: corners of triangles of area 0.0035 or more. `edge_tris`: the two triangles of edge m differ and both lie in [256 (m // 256), 256 (m // 256) + 256); in each such block every triangle is the plus triangle of exactly one edge. pivots[p, i] is 256 p + i or at least 256 (p + 1); the entries of pivots[p] are distinct. `lower_inv`: each panel's complex matrix is lower triangular with unit diagonal. `upper_inv`: each panel's complex matrix is upper triangular with diagonal entries of modulus 0.5 to 2.
All inputs are finite; a program needn't handle non-finite values.
Results may differ from a plain program's by a relative error of at most 0.0003.
Values sent between devices are 32-bit elements; how exact they have to be, the bound alone decides.
No kernel may reach another device: no remote copies, remote signals or barrier semaphores. Data moves between devices by JAX's collectives and lax.ppermute only.
A program may use at most 64 MiB of HBM per device.

v0:
```python
import math
import jax
import jax.numpy as jnp
from jax import lax
from jax.sharding import PartitionSpec as P

SLAB = 512
PW = 256
wave_number = 2.0 * math.pi
core_square = 0.0025
edge_square = 0.0225
quad_bary = (
    (1.0 / 3.0, 1.0 / 3.0, 1.0 / 3.0),
    (0.05971587178977, 0.470142064105115, 0.470142064105115),
    (0.470142064105115, 0.05971587178977, 0.470142064105115),
    (0.470142064105115, 0.470142064105115, 0.05971587178977),
    (0.797426985353087, 0.101286507323456, 0.101286507323456),
    (0.101286507323456, 0.797426985353087, 0.101286507323456),
    (0.101286507323456, 0.101286507323456, 0.797426985353087),
)
quad_weight = (
    0.225,
    0.132394152788506,
    0.132394152788506,
    0.132394152788506,
    0.125939180544827,
    0.125939180544827,
    0.125939180544827,
)


def broadcast(block, axis, owner):
    block = jnp.where(lax.axis_index(axis) == owner, block, jnp.zeros_like(block))
    return lax.psum(block, axis)


def exact_dot(first_matrix, second_matrix):
    return jnp.dot(first_matrix, second_matrix, precision=lax.Precision.HIGHEST)


def complex_dot(first_real, first_imag, second_real, second_imag):
    out_real = exact_dot(first_real, second_real) - exact_dot(first_imag, second_imag)
    out_imag = exact_dot(first_real, second_imag) + exact_dot(first_imag, second_real)
    return (out_real, out_imag)


def triangle_data(corners, free_index):
    total_count = corners.shape[1]
    vertex = corners.reshape(3, 3, total_count)
    choose = (free_index[None, :] == jnp.arange(3, dtype=jnp.int32)[:, None]).astype(corners.dtype)
    free_vertex = jnp.sum(choose[:, None, :] * vertex, axis=0)
    after_one = jnp.sum(jnp.roll(choose, 1, axis=0)[:, None, :] * vertex, axis=0)
    after_two = jnp.sum(jnp.roll(choose, 2, axis=0)[:, None, :] * vertex, axis=0)
    edge_side = after_one - after_two
    length = jnp.sqrt(jnp.sum(edge_side * edge_side, axis=0))
    normal = jnp.cross(vertex[1] - vertex[0], vertex[2] - vertex[0], axis=0)
    tri_area = 0.5 * jnp.sqrt(jnp.sum(normal * normal, axis=0))
    points = jnp.stack(
        [
            quad_bary[point_index][0] * vertex[0]
            + quad_bary[point_index][1] * vertex[1]
            + quad_bary[point_index][2] * vertex[2]
            for point_index in range(7)
        ],
        axis=1,
    )
    return (points, free_vertex, length, tri_area)


def edge_geometry(plus_corners, minus_corners, plus_free, minus_free):
    plus_points, plus_vertex, length, plus_area = triangle_data(plus_corners, plus_free)
    minus_points, minus_vertex, spare_length, minus_area = triangle_data(minus_corners, minus_free)
    weight = jnp.array(quad_weight, dtype=plus_area.dtype)[:, None]
    plus_vec = (length / (2.0 * plus_area))[None, None, :] * (plus_points - plus_vertex[:, None, :])
    minus_vec = (length / (2.0 * minus_area))[None, None, :] * (
        minus_vertex[:, None, :] - minus_points
    )
    points = jnp.stack([plus_points, minus_points])
    vectors = jnp.stack([plus_vec, minus_vec])
    divergence = jnp.stack([length / plus_area, -length / minus_area])
    weighted = jnp.stack([weight * plus_area[None, :], weight * minus_area[None, :]])
    return (points, vectors, divergence, weighted)


def fill_block(test_geometry, source_geometry):
    test_points, test_vectors, test_div, test_weight = test_geometry
    source_points, source_vectors, source_div, source_weight = source_geometry
    row_count = test_div.shape[1]
    col_count = source_div.shape[1]

    def one_point(point_index, totals):
        real_sum, imag_sum = totals
        for test_sign in range(2):
            here = lax.dynamic_index_in_dim(test_points[test_sign], point_index, 1, keepdims=False)
            along = lax.dynamic_index_in_dim(
                test_vectors[test_sign], point_index, 1, keepdims=False
            )
            test_scale = lax.dynamic_index_in_dim(
                test_weight[test_sign], point_index, 0, keepdims=False
            )
            for source_sign in range(2):
                there = source_points[source_sign]
                other = source_vectors[source_sign]
                gap_x = here[0][None, :, None] - there[0][:, None, :]
                gap_y = here[1][None, :, None] - there[1][:, None, :]
                gap_z = here[2][None, :, None] - there[2][:, None, :]
                distance = jnp.sqrt(gap_x * gap_x + gap_y * gap_y + gap_z * gap_z + core_square)
                inner_product = (
                    along[0][None, :, None] * other[0][:, None, :]
                    + along[1][None, :, None] * other[1][:, None, :]
                    + along[2][None, :, None] * other[2][:, None, :]
                )
                factor = (
                    wave_number * inner_product
                    - test_div[test_sign][None, :, None]
                    * source_div[source_sign][None, None, :]
                    / wave_number
                )
                factor = (
                    factor
                    * (test_scale[None, :, None] * source_weight[source_sign][:, None, :])
                    / (edge_square * distance)
                )
                phase_angle = wave_number * distance
                real_sum = real_sum + jnp.sum(factor * jnp.sin(phase_angle), axis=0)
                imag_sum = imag_sum + jnp.sum(factor * jnp.cos(phase_angle), axis=0)
        return (real_sum, imag_sum)

    empty_sum = jnp.zeros((row_count, col_count), dtype=test_div.dtype)
    return lax.fori_loop(0, 7, one_point, (empty_sum, empty_sum))


def pick_columns(table, local_index):
    table_width = table.shape[1]
    onehot = (jnp.arange(table_width, dtype=jnp.int32)[:, None] == local_index[None, :]).astype(
        jnp.float32
    )
    return exact_dot(table, onehot)


def per_device(tri_corners, edge_tris, edge_free, pivots, lower_inv, upper_inv):
    row_count = edge_tris.shape[1]
    grid_row = lax.axis_index("prow")
    grid_col = lax.axis_index("pcol")
    per_column = SLAB // lax.axis_size("pcol")
    row_block = lax.all_gather(tri_corners, "pcol", axis=1, tiled=True)
    row_base = grid_row * row_count
    test_geometry = edge_geometry(
        pick_columns(row_block, edge_tris[0] - row_base),
        pick_columns(row_block, edge_tris[1] - row_base),
        edge_free[0],
        edge_free[1],
    )
    root_row = grid_col * per_column // row_count
    shared = broadcast(row_block, "prow", root_row)
    tables = broadcast(jnp.concatenate([edge_tris, edge_free], axis=0), "prow", root_row)
    col_base = root_row * row_count
    chosen = lax.dynamic_slice_in_dim(tables, grid_col * per_column - col_base, per_column, 1)
    plus_cols = pick_columns(shared, chosen[0] - col_base)
    minus_cols = pick_columns(shared, chosen[1] - col_base)
    plus_free = chosen[2]
    minus_free = chosen[3]
    source_geometry = edge_geometry(plus_cols, minus_cols, plus_free, minus_free)
    real_part, imag_part = fill_block(test_geometry, source_geometry)
    local_tile = jnp.concatenate([real_part, imag_part], axis=1)
    lower_all, upper_all = (
        lax.all_gather(lower_inv, "prow", axis=2, tiled=True),
        lax.all_gather(upper_inv, "prow", axis=2, tiled=True),
    )
    global_rows = row_base + jnp.arange(row_count, dtype=jnp.int32)
    global_cols = grid_col * per_column + jnp.arange(per_column, dtype=jnp.int32)
    slot_ids = jnp.arange(PW, dtype=jnp.int32)
    finish = PW
    owner_row = 0 // row_count
    pivot_rows = pivots[0]
    select = (pivot_rows[:, None] == global_rows[None, :]).astype(jnp.float32)
    incoming_part = exact_dot(select, local_tile)
    local_start = 0 - owner_row * row_count
    diagonal_part = local_tile[local_start : local_start + PW]
    incoming = lax.psum(incoming_part, "prow")
    initial = broadcast(diagonal_part, "prow", owner_row)
    moved_rows = (
        (global_rows[:, None] == pivot_rows[None, :])
        & (pivot_rows[None, :] != 0 + slot_ids[None, :])
    ).astype(jnp.float32)
    swapped_in = exact_dot(moved_rows, initial)
    was_moved = jnp.sum(moved_rows, axis=1) > 0.5
    on_diagonal = (global_rows[:, None] == 0 + slot_ids[None, :]).astype(jnp.float32)
    from_pivots = exact_dot(on_diagonal, incoming)
    in_block = (global_rows >= 0) & (global_rows < finish)
    local_tile = jnp.where(
        in_block[:, None], from_pivots, jnp.where(was_moved[:, None], swapped_in, local_tile)
    )
    padded = lax.dynamic_update_slice(
        jnp.zeros((2, SLAB, PW), jnp.float32), upper_all[0], (0, 0, 0)
    )
    segment = lax.all_gather(local_tile, "pcol", axis=1, tiled=True)
    shards = segment.shape[1] // (2 * per_column)
    shaped = segment.reshape(row_count, shards, 2, per_column)
    segment_real = shaped[:, :, 0, :].reshape(row_count, shards * per_column)
    segment_imag = shaped[:, :, 1, :].reshape(row_count, shards * per_column)
    weights = lax.dynamic_slice_in_dim(padded, jnp.int32(0) // 2, shards * per_column, 1)
    out_real, out_imag = complex_dot(segment_real, segment_imag, weights[0], weights[1])
    left_factor = jnp.zeros((row_count, 2 * PW), jnp.float32) + jnp.concatenate(
        [out_real, out_imag], axis=1
    )
    lower_now = lower_all[0]
    right_real, right_imag = complex_dot(
        lower_now[0], lower_now[1], incoming[:, :per_column], incoming[:, per_column:]
    )
    left_real = left_factor[:, :PW]
    left_imag = left_factor[:, PW:]
    update_real, update_imag = complex_dot(left_real, left_imag, right_real, right_imag)
    col_offset = jnp.clip(grid_col * per_column - 0, 0, PW - per_column)
    panel_real = lax.dynamic_slice_in_dim(left_real, col_offset, per_column, 1)
    panel_imag = lax.dynamic_slice_in_dim(left_imag, col_offset, per_column, 1)
    below = global_rows >= finish
    trailing = below[:, None] & (global_cols >= finish)[None, :]
    in_panel = below[:, None] & ((global_cols >= 0) & (global_cols < finish))[None, :]
    tile_real = local_tile[:, :per_column]
    tile_imag = local_tile[:, per_column:]
    new_real = jnp.where(
        trailing, tile_real - update_real, jnp.where(in_panel, panel_real, tile_real)
    )
    new_imag = jnp.where(
        trailing, tile_imag - update_imag, jnp.where(in_panel, panel_imag, tile_imag)
    )
    local_tile = jnp.concatenate([new_real, new_imag], axis=1)
    return local_tile


def solution(mesh):
    in_specs = (
        P(None, ("prow", "pcol")),
        P(None, "prow"),
        P(None, "prow"),
        P(),
        P(None, None, "prow", None),
        P(None, None, "prow", None),
    )
    out_specs = P("prow", "pcol")
    return jax.shard_map(
        per_device, mesh=mesh, in_specs=in_specs, out_specs=out_specs, check_vma=False
    )
```

profile of v0, /device:TPU:0, one launch (start us, length us, event | category | flops | bytes accessed | tf_op | source)
XLA Modules:
  0.0 290.3 jit_solution(5166626255349097872)
XLA Ops:
  7.9 10.7 %psum.28 = s32[4,256]{1,0:T(4,128)S(1)} all-reduce(s32[4,256]{1,0:T(4,128)S(1)} %add_select_fusion), channel_id=1, replica_groups=mesh['prow'=8,'pcol'=4] {'prow'}, use_global_device_ids=true, to_apply=%region_6.8 | all-reduce | flops 1024 | bytes 8192 | tf_op jit(solution)/shard_map/psum | solution.py:34
  19.3 8.2 %all-gather = f32[4,64,9]{1,2,0:T(8,128)S(1)} all-gather(f32[1,64,9]{1,2,0:T(8,128)S(1)} %bitcast.272), channel_id=1, replica_groups=mesh['prow'=8,'pcol'=4] {'pcol'}, dimensions={0}, use_global_device_ids=true | all-gather | bytes 11520 | tf_op jit(solution)/shard_map/all_gather | solution.py:146
  27.9 25.9 %psum.29 = f32[9,256]{1,0:T(8,128)S(1)} all-reduce(f32[9,256]{1,0:T(8,128)S(1)} %select_bitcast_fusion), channel_id=1, replica_groups=mesh['prow'=8,'pcol'=4] {'prow'}, use_global_device_ids=true, to_apply=%region_5.7 | all-reduce | flops 2304 | bytes 18432 | tf_op jit(solution)/shard_map/psum | solution.py:34
  56.0 128.9 %while.18 = (s32[]{:T(128)}, f32[256,128]{1,0:T(8,128)S(1)}, f32[256,128]{1,0:T(8,128)S(1)}, f32[3,7,256]{2,1,0:T(8,128)S(1)}, f32[3,7,128]{2,1,0:T(8,128)S(1)},...) while((s32[]{:T(128)}, f32[256,128]{1,0:T(8,128)S(1)}, ...), condition=%wide.region_25.28_spmd.clone.clone.clone, body=%wide.region_16.27_spmd.clone.clone.clone.sunk | while | flops 23267076 | bytes 3925331 | solution.py:130
  56.4 4.5 %multiply_reduce_fusion.22 = (f32[256,128]{1,0:T(8,128)S(1)}, f32[256,128]{1,0:T(8,128)S(1)}) fusion(f32[256]{0:T(256)S(1)} %bitcast.245, f32[256]{0:T(256)S(1)} %bitcast.243, f32[256]{0:T(256)S(1)} %bitcast.241, f32[7,128]{1,0:T(8,128)S(1)} %get-tuple-element.879, f32[7,128]{1,0:T(8,128)S(1)} %get-tuple-element.880, ...), kind=kLoop, calls=%fused_computation.2.clone.1 | loop fusion | flops 5668864 | bytes 425472 | tf_op jit(solution)/shard_map/while/body/eval_jaxpr/reduce_sum | solution.py:126
  60.8 4.5 %multiply_reduce_fusion.24 = (f32[256,128]{1,0:T(8,128)S(1)}, f32[256,128]{1,0:T(8,128)S(1)}) fusion(f32[7,128]{1,0:T(8,128)S(1)} %get-tuple-element.879, f32[7,128]{1,0:T(8,128)S(1)} %get-tuple-element.880, f32[7,128]{1,0:T(8,128)S(1)} %get-tuple-element.881, f32[256]{0:T(256)S(1)} %bitcast.257, f32[256]{0:T(256)S(1)} %bitcast.255, ...), kind=kLoop, calls=%fused_computation.4.clone.1 | loop fusion | flops 5668864 | bytes 425472 | tf_op jit(solution)/shard_map/while/body/eval_jaxpr/reduce_sum | solution.py:126
  65.3 4.5 %multiply_reduce_fusion.25 = (f32[256,128]{1,0:T(8,128)S(1)}, f32[256,128]{1,0:T(8,128)S(1)}) fusion(f32[7,128]{1,0:T(8,128)S(1)} %get-tuple-element.891, f32[256]{0:T(256)S(1)} %bitcast.258, f32[7,128]{1,0:T(8,128)S(1)} %get-tuple-element.892, f32[256]{0:T(256)S(1)} %bitcast.256, f32[7,128]{1,0:T(8,128)S(1)} %get-tuple-element.893, ...), kind=kLoop, calls=%fused_computation.5.clone.1 | loop fusion | flops 5668864 | bytes 425472 | tf_op jit(solution)/shard_map/while/body/eval_jaxpr/reduce_sum | solution.py:126
  69.8 4.5 %multiply_reduce_fusion.23 = (f32[256,128]{1,0:T(8,128)S(1)}, f32[256,128]{1,0:T(8,128)S(1)}) fusion(f32[256]{0:T(256)S(1)} %bitcast.246, f32[256]{0:T(256)S(1)} %bitcast.244, f32[256]{0:T(256)S(1)} %bitcast.242, f32[7,128]{1,0:T(8,128)S(1)} %get-tuple-element.891, f32[7,128]{1,0:T(8,128)S(1)} %get-tuple-element.892, ...), kind=kLoop, calls=%fused_computation.3.clone.1 | loop fusion | flops 5668864 | bytes 425472 | tf_op jit(solution)/shard_map/while/body/eval_jaxpr/reduce_sum | solution.py:126
  74.8 4.5 %multiply_reduce_fusion.22 = (f32[256,128]{1,0:T(8,128)S(1)}, f32[256,128]{1,0:T(8,128)S(1)}) fusion(f32[256]{0:T(256)S(1)} %bitcast.245, f32[256]{0:T(256)S(1)} %bitcast.243, f32[256]{0:T(256)S(1)} %bitcast.241, f32[7,128]{1,0:T(8,128)S(1)} %get-tuple-element.879, f32[7,128]{1,0:T(8,128)S(1)} %get-tuple-element.880, ...), kind=kLoop, calls=%fused_computation.2.clone.1 | loop fusion | flops 5668864 | bytes 425472 | tf_op jit(solution)/shard_map/while/body/eval_jaxpr/reduce_sum | solution.py:126
  79.3 4.5 %multiply_reduce_fusion.24 = (f32[256,128]{1,0:T(8,128)S(1)}, f32[256,128]{1,0:T(8,128)S(1)}) fusion(f32[7,128]{1,0:T(8,128)S(1)} %get-tuple-element.879, f32[7,128]{1,0:T(8,128)S(1)} %get-tuple-element.880, f32[7,128]{1,0:T(8,128)S(1)} %get-tuple-element.881, f32[256]{0:T(256)S(1)} %bitcast.257, f32[256]{0:T(256)S(1)} %bitcast.255, ...), kind=kLoop, calls=%fused_computation.4.clone.1 | loop fusion | flops 5668864 | bytes 425472 | tf_op jit(solution)/shard_map/while/body/eval_jaxpr/reduce_sum | solution.py:126
  83.7 4.5 %multiply_reduce_fusion.25 = (f32[256,128]{1,0:T(8,128)S(1)}, f32[256,128]{1,0:T(8,128)S(1)}) fusion(f32[7,128]{1,0:T(8,128)S(1)} %get-tuple-element.891, f32[256]{0:T(256)S(1)} %bitcast.258, f32[7,128]{1,0:T(8,128)S(1)} %get-tuple-element.892, f32[256]{0:T(256)S(1)} %bitcast.256, f32[7,128]{1,0:T(8,128)S(1)} %get-tuple-element.893, ...), kind=kLoop, calls=%fused_computation.5.clone.1 | loop fusion | flops 5668864 | bytes 425472 | tf_op jit(solution)/shard_map/while/body/eval_jaxpr/reduce_sum | solution.py:126
  88.2 4.5 %multiply_reduce_fusion.23 = (f32[256,128]{1,0:T(8,128)S(1)}, f32[256,128]{1,0:T(8,128)S(1)}) fusion(f32[256]{0:T(256)S(1)} %bitcast.246, f32[256]{0:T(256)S(1)} %bitcast.244, f32[256]{0:T(256)S(1)} %bitcast.242, f32[7,128]{1,0:T(8,128)S(1)} %get-tuple-element.891, f32[7,128]{1,0:T(8,128)S(1)} %get-tuple-element.892, ...), kind=kLoop, calls=%fused_computation.3.clone.1 | loop fusion | flops 5668864 | bytes 425472 | tf_op jit(solution)/shard_map/while/body/eval_jaxpr/reduce_sum | solution.py:126
  93.2 4.5 %multiply_reduce_fusion.22 = (f32[256,128]{1,0:T(8,128)S(1)}, f32[256,128]{1,0:T(8,128)S(1)}) fusion(f32[256]{0:T(256)S(1)} %bitcast.245, f32[256]{0:T(256)S(1)} %bitcast.243, f32[256]{0:T(256)S(1)} %bitcast.241, f32[7,128]{1,0:T(8,128)S(1)} %get-tuple-element.879, f32[7,128]{1,0:T(8,128)S(1)} %get-tuple-element.880, ...), kind=kLoop, calls=%fused_computation.2.clone.1 | loop fusion | flops 5668864 | bytes 425472 | tf_op jit(solution)/shard_map/while/body/eval_jaxpr/reduce_sum | solution.py:126
  97.7 4.5 %multiply_reduce_fusion.24 = (f32[256,128]{1,0:T(8,128)S(1)}, f32[256,128]{1,0:T(8,128)S(1)}) fusion(f32[7,128]{1,0:T(8,128)S(1)} %get-tuple-element.879, f32[7,128]{1,0:T(8,128)S(1)} %get-tuple-element.880, f32[7,128]{1,0:T(8,128)S(1)} %get-tuple-element.881, f32[256]{0:T(256)S(1)} %bitcast.257, f32[256]{0:T(256)S(1)} %bitcast.255, ...), kind=kLoop, calls=%fused_computation.4.clone.1 | loop fusion | flops 5668864 | bytes 425472 | tf_op jit(solution)/shard_map/while/body/eval_jaxpr/reduce_sum | solution.py:126
  106.6 4.5 %multiply_reduce_fusion.23 = (f32[256,128]{1,0:T(8,128)S(1)}, f32[256,128]{1,0:T(8,128)S(1)}) fusion(f32[256]{0:T(256)S(1)} %bitcast.246, f32[256]{0:T(256)S(1)} %bitcast.244, f32[256]{0:T(256)S(1)} %bitcast.242, f32[7,128]{1,0:T(8,128)S(1)} %get-tuple-element.891, f32[7,128]{1,0:T(8,128)S(1)} %get-tuple-element.892, ...), kind=kLoop, calls=%fused_computation.3.clone.1 | loop fusion | flops 5668864 | bytes 425472 | tf_op jit(solution)/shard_map/while/body/eval_jaxpr/reduce_sum | solution.py:126
  111.6 4.5 %multiply_reduce_fusion.22 = (f32[256,128]{1,0:T(8,128)S(1)}, f32[256,128]{1,0:T(8,128)S(1)}) fusion(f32[256]{0:T(256)S(1)} %bitcast.245, f32[256]{0:T(256)S(1)} %bitcast.243, f32[256]{0:T(256)S(1)} %bitcast.241, f32[7,128]{1,0:T(8,128)S(1)} %get-tuple-element.879, f32[7,128]{1,0:T(8,128)S(1)} %get-tuple-element.880, ...), kind=kLoop, calls=%fused_computation.2.clone.1 | loop fusion | flops 5668864 | bytes 425472 | tf_op jit(solution)/shard_map/while/body/eval_jaxpr/reduce_sum | solution.py:126
  116.1 4.5 %multiply_reduce_fusion.24 = (f32[256,128]{1,0:T(8,128)S(1)}, f32[256,128]{1,0:T(8,128)S(1)}) fusion(f32[7,128]{1,0:T(8,128)S(1)} %get-tuple-element.879, f32[7,128]{1,0:T(8,128)S(1)} %get-tuple-element.880, f32[7,128]{1,0:T(8,128)S(1)} %get-tuple-element.881, f32[256]{0:T(256)S(1)} %bitcast.257, f32[256]{0:T(256)S(1)} %bitcast.255, ...), kind=kLoop, calls=%fused_computation.4.clone.1 | loop fusion | flops 5668864 | bytes 425472 | tf_op jit(solution)/shard_map/while/body/eval_jaxpr/reduce_sum | solution.py:126
  125.1 4.5 %multiply_reduce_fusion.23 = (f32[256,128]{1,0:T(8,128)S(1)}, f32[256,128]{1,0:T(8,128)S(1)}) fusion(f32[256]{0:T(256)S(1)} %bitcast.246, f32[256]{0:T(256)S(1)} %bitcast.244, f32[256]{0:T(256)S(1)} %bitcast.242, f32[7,128]{1,0:T(8,128)S(1)} %get-tuple-element.891, f32[7,128]{1,0:T(8,128)S(1)} %get-tuple-element.892, ...), kind=kLoop, calls=%fused_computation.3.clone.1 | loop fusion | flops 5668864 | bytes 425472 | tf_op jit(solution)/shard_map/while/body/eval_jaxpr/reduce_sum | solution.py:126
  130.1 4.5 %multiply_reduce_fusion.22 = (f32[256,128]{1,0:T(8,128)S(1)}, f32[256,128]{1,0:T(8,128)S(1)}) fusion(f32[256]{0:T(256)S(1)} %bitcast.245, f32[256]{0:T(256)S(1)} %bitcast.243, f32[256]{0:T(256)S(1)} %bitcast.241, f32[7,128]{1,0:T(8,128)S(1)} %get-tuple-element.879, f32[7,128]{1,0:T(8,128)S(1)} %get-tuple-element.880, ...), kind=kLoop, calls=%fused_computation.2.clone.1 | loop fusion | flops 5668864 | bytes 425472 | tf_op jit(solution)/shard_map/while/body/eval_jaxpr/reduce_sum | solution.py:126
  134.5 4.5 %multiply_reduce_fusion.24 = (f32[256,128]{1,0:T(8,128)S(1)}, f32[256,128]{1,0:T(8,128)S(1)}) fusion(f32[7,128]{1,0:T(8,128)S(1)} %get-tuple-element.879, f32[7,128]{1,0:T(8,128)S(1)} %get-tuple-element.880, f32[7,128]{1,0:T(8,128)S(1)} %get-tuple-element.881, f32[256]{0:T(256)S(1)} %bitcast.257, f32[256]{0:T(256)S(1)} %bitcast.255, ...), kind=kLoop, calls=%fused_computation.4.clone.1 | loop fusion | flops 5668864 | bytes 425472 | tf_op jit(solution)/shard_map/while/body/eval_jaxpr/reduce_sum | solution.py:126
  139.0 4.5 %multiply_reduce_fusion.25 = (f32[256,128]{1,0:T(8,128)S(1)}, f32[256,128]{1,0:T(8,128)S(1)}) fusion(f32[7,128]{1,0:T(8,128)S(1)} %get-tuple-element.891, f32[256]{0:T(256)S(1)} %bitcast.258, f32[7,128]{1,0:T(8,128)S(1)} %get-tuple-element.892, f32[256]{0:T(256)S(1)} %bitcast.256, f32[7,128]{1,0:T(8,128)S(1)} %get-tuple-element.893, ...), kind=kLoop, calls=%fused_computation.5.clone.1 | loop fusion | flops 5668864 | bytes 425472 | tf_op jit(solution)/shard_map/while/body/eval_jaxpr/reduce_sum | solution.py:126
  143.5 4.5 %multiply_reduce_fusion.23 = (f32[256,128]{1,0:T(8,128)S(1)}, f32[256,128]{1,0:T(8,128)S(1)}) fusion(f32[256]{0:T(256)S(1)} %bitcast.246, f32[256]{0:T(256)S(1)} %bitcast.244, f32[256]{0:T(256)S(1)} %bitcast.242, f32[7,128]{1,0:T(8,128)S(1)} %get-tuple-element.891, f32[7,128]{1,0:T(8,128)S(1)} %get-tuple-element.892, ...), kind=kLoop, calls=%fused_computation.3.clone.1 | loop fusion | flops 5668864 | bytes 425472 | tf_op jit(solution)/shard_map/while/body/eval_jaxpr/reduce_sum | solution.py:126
  148.5 4.5 %multiply_reduce_fusion.22 = (f32[256,128]{1,0:T(8,128)S(1)}, f32[256,128]{1,0:T(8,128)S(1)}) fusion(f32[256]{0:T(256)S(1)} %bitcast.245, f32[256]{0:T(256)S(1)} %bitcast.243, f32[256]{0:T(256)S(1)} %bitcast.241, f32[7,128]{1,0:T(8,128)S(1)} %get-tuple-element.879, f32[7,128]{1,0:T(8,128)S(1)} %get-tuple-element.880, ...), kind=kLoop, calls=%fused_computation.2.clone.1 | loop fusion | flops 5668864 | bytes 425472 | tf_op jit(solution)/shard_map/while/body/eval_jaxpr/reduce_sum | solution.py:126
  153.0 4.5 %multiply_reduce_fusion.24 = (f32[256,128]{1,0:T(8,128)S(1)}, f32[256,128]{1,0:T(8,128)S(1)}) fusion(f32[7,128]{1,0:T(8,128)S(1)} %get-tuple-element.879, f32[7,128]{1,0:T(8,128)S(1)} %get-tuple-element.880, f32[7,128]{1,0:T(8,128)S(1)} %get-tuple-element.881, f32[256]{0:T(256)S(1)} %bitcast.257, f32[256]{0:T(256)S(1)} %bitcast.255, ...), kind=kLoop, calls=%fused_computation.4.clone.1 | loop fusion | flops 5668864 | bytes 425472 | tf_op jit(solution)/shard_map/while/body/eval_jaxpr/reduce_sum | solution.py:126
  157.4 4.5 %multiply_reduce_fusion.25 = (f32[256,128]{1,0:T(8,128)S(1)}, f32[256,128]{1,0:T(8,128)S(1)}) fusion(f32[7,128]{1,0:T(8,128)S(1)} %get-tuple-element.891, f32[256]{0:T(256)S(1)} %bitcast.258, f32[7,128]{1,0:T(8,128)S(1)} %get-tuple-element.892, f32[256]{0:T(256)S(1)} %bitcast.256, f32[7,128]{1,0:T(8,128)S(1)} %get-tuple-element.893, ...), kind=kLoop, calls=%fused_computation.5.clone.1 | loop fusion | flops 5668864 | bytes 425472 | tf_op jit(solution)/shard_map/while/body/eval_jaxpr/reduce_sum | solution.py:126
  161.9 4.5 %multiply_reduce_fusion.23 = (f32[256,128]{1,0:T(8,128)S(1)}, f32[256,128]{1,0:T(8,128)S(1)}) fusion(f32[256]{0:T(256)S(1)} %bitcast.246, f32[256]{0:T(256)S(1)} %bitcast.244, f32[256]{0:T(256)S(1)} %bitcast.242, f32[7,128]{1,0:T(8,128)S(1)} %get-tuple-element.891, f32[7,128]{1,0:T(8,128)S(1)} %get-tuple-element.892, ...), kind=kLoop, calls=%fused_computation.3.clone.1 | loop fusion | flops 5668864 | bytes 425472 | tf_op jit(solution)/shard_map/while/body/eval_jaxpr/reduce_sum | solution.py:126
  166.9 4.5 %multiply_reduce_fusion.22 = (f32[256,128]{1,0:T(8,128)S(1)}, f32[256,128]{1,0:T(8,128)S(1)}) fusion(f32[256]{0:T(256)S(1)} %bitcast.245, f32[256]{0:T(256)S(1)} %bitcast.243, f32[256]{0:T(256)S(1)} %bitcast.241, f32[7,128]{1,0:T(8,128)S(1)} %get-tuple-element.879, f32[7,128]{1,0:T(8,128)S(1)} %get-tuple-element.880, ...), kind=kLoop, calls=%fused_computation.2.clone.1 | loop fusion | flops 5668864 | bytes 425472 | tf_op jit(solution)/shard_map/while/body/eval_jaxpr/reduce_sum | solution.py:126
  171.4 4.5 %multiply_reduce_fusion.24 = (f32[256,128]{1,0:T(8,128)S(1)}, f32[256,128]{1,0:T(8,128)S(1)}) fusion(f32[7,128]{1,0:T(8,128)S(1)} %get-tuple-element.879, f32[7,128]{1,0:T(8,128)S(1)} %get-tuple-element.880, f32[7,128]{1,0:T(8,128)S(1)} %get-tuple-element.881, f32[256]{0:T(256)S(1)} %bitcast.257, f32[256]{0:T(256)S(1)} %bitcast.255, ...), kind=kLoop, calls=%fused_computation.4.clone.1 | loop fusion | flops 5668864 | bytes 425472 | tf_op jit(solution)/shard_map/while/body/eval_jaxpr/reduce_sum | solution.py:126
  175.9 4.5 %multiply_reduce_fusion.25 = (f32[256,128]{1,0:T(8,128)S(1)}, f32[256,128]{1,0:T(8,128)S(1)}) fusion(f32[7,128]{1,0:T(8,128)S(1)} %get-tuple-element.891, f32[256]{0:T(256)S(1)} %bitcast.258, f32[7,128]{1,0:T(8,128)S(1)} %get-tuple-element.892, f32[256]{0:T(256)S(1)} %bitcast.256, f32[7,128]{1,0:T(8,128)S(1)} %get-tuple-element.893, ...), kind=kLoop, calls=%fused_computation.5.clone.1 | loop fusion | flops 5668864 | bytes 425472 | tf_op jit(solution)/shard_map/while/body/eval_jaxpr/reduce_sum | solution.py:126
  188.1 53.6 %all-reduce.4.cloned.1.call-done = (f32[256,256]{1,0:T(8,128)}, f32[256,256]{0,1:T(8,128)}) async-done(((f32[256,256]{1,0:T(8,128)}, f32[256,256]{0,1:T(8,128)}), (f32[256,256]{1,0:T(8,128)}, f32[256,256]{0,1:T(8,128)})) %all-reduce.4.cloned.1.call-update) | async-done | bytes 524304 | tf_op jit(solution)/shard_map/psum | solution.py:180
  245.1 15.0 %all_gather.15 = f32[1,2,256,256]{3,2,1,0:T(8,128)S(1)} all-gather(f32[1,2,32,256]{3,2,1,0:T(8,128)S(1)} %copy-done.3), channel_id=1, replica_groups=mesh['prow'=8,'pcol'=4] {'prow'}, dimensions={2}, use_global_device_ids=true | all-gather | bytes 589824 | tf_op jit(solution)/shard_map/all_gather | solution.py:167
  260.1 14.9 %all_gather.14 = f32[1,2,256,256]{3,2,1,0:T(8,128)S(1)} all-gather(f32[1,2,32,256]{3,2,1,0:T(8,128)S(1)} %copy-done.4), channel_id=1, replica_groups=mesh['prow'=8,'pcol'=4] {'prow'}, dimensions={2}, use_global_device_ids=true | all-gather | bytes 589824 | tf_op jit(solution)/shard_map/all_gather | solution.py:168
  (234 shorter events, 35.7 us)
Async XLA Ops:
  6.5 235.2 %all-reduce.4.cloned.1.call-start = ((), (), s32[]{:S(2)}) async-start(), calls=%async_computation.1 | async-start | bytes 1048576 | tf_op jit(solution)/shard_map/psum | solution.py:180
  6.5 0.7 copy-start.8
  7.2 0.7 copy-start.9
  18.6 0.7 copy-start.7
  55.3 0.7 copy-start.5
  185.9 0.7 copy-start.6
  187.7 89.0 %all-gather.3.cloned.1.call-start = ((), (), s32[]{:S(2)}) async-start(), calls=%async_computation | async-start | bytes 1310720 | tf_op jit(solution)/shard_map/all_gather | solution.py:197
  241.7 1.4 copy-start.2
  244.3 0.8 copy-start.3
  245.1 15.0 %copy-start.4 = (f32[1,2,32,256]{3,2,1,0:T(8,128)S(1)}, f32[1,2,32,256]{3,2,1,0:T(8,128)}, u32[]{:S(2)}) copy-start(f32[1,2,32,256]{3,2,1,0:T(8,128)} %param.19) | copy-start | bytes 196612
  260.1 14.9 %copy-start.1 = (f32[256,256]{1,0:T(8,128)S(1)}, f32[256,256]{1,0:T(8,128)}, u32[]{:S(2)}) copy-start(f32[256,256]{1,0:T(8,128)} %get-tuple-element.613) | copy-start | bytes 786436
  281.0 1.0 copy-start
Sparse Core Ops, SparseCore 0:
  187.8 53.9 all-reduce.3
  244.4 25.5 all-gather.2
where the time goes:
time: 291 us; the launch traced here: 290 us
  other arithmetic  129 us (44%)
  blocking collectives  74.6 us (26%)
  waiting for transfers between devices  53.6 us (18%)
  between operations  14 us (5%)
  matrix products  9.77 us (3%)
  local copies, waits for them, and re-layouts  7.87 us (3%)
    reduce_sum x28, other arithmetic, one_point(): imag_sum = imag_sum + jnp.sum(factor * jnp.cos(phase_angle), axis=0)  125 us
    psum x1, waiting for transfers between devices, per_device(): incoming = lax.psum(incoming_part, 'prow')  53.6 us
    psum x2, blocking collectives, broadcast(): return lax.psum(block, axis)  36.6 us
    all_gather x1, blocking collectives, per_device(): lax.all_gather(lower_inv, 'prow', axis=2, tiled=True)  15 us
    all_gather x1, blocking collectives, per_device(): lax.all_gather(upper_inv, 'prow', axis=2, tiled=True)  14.9 us
    dot_general x19, matrix products, exact_dot(): return jnp.dot(first_matrix, second_matrix, precision=lax.Precision.HIGHEST)  9.77 us
    all_gather x1, blocking collectives, per_device(): row_block = lax.all_gather(tri_corners, 'pcol', axis=1, tiled=True)  8.18 us
  transfers between devices with their start and end apart: 2, of which 1 were waited for; matrix products, arithmetic and copies ran while one was open for 1% of the time, Pallas kernels for 0%

commit v1 on v0

--- a/solution.py
+++ b/solution.py
@@ -177,7 +177,9 @@
     incoming_part = exact_dot(select, local_tile)
     local_start = 0 - owner_row * row_count
     diagonal_part = local_tile[local_start : local_start + PW]
-    incoming = lax.psum(incoming_part, "prow")
+    incoming = incoming_part
+    for hop in (1, 2, 4):
+        incoming = incoming + lax.ppermute(incoming, "prow", [(dev, dev ^ hop) for dev in range(8)])
     initial = broadcast(diagonal_part, "prow", owner_row)
     moved_rows = (
         (global_rows[:, None] == pivot_rows[None, :])

time: 291 us -> 294 us (1.010)
  waiting for transfers between devices: 53.6 us -> 58.1 us
    ppermute x0 -> x3, waiting for transfers between devices: none -> 9.35 us  [per_device(): lax.ppermute(incoming, 'prow', [(dev, dev ^ hop) for dev in range(8)])]
    psum x1, waiting for transfers between devices: 53.6 us -> 48.7 us  [broadcast(): return lax.psum(block, axis)]
  transfers between devices with their start and end apart: 2 -> 5, of which waited for: 1 -> 3; matrix products, arithmetic and copies ran while one was open for 1% -> 1% of each run, Pallas kernels for 0% -> 0%
where the time goes in v1:
time: 294 us
  other arithmetic  129 us (44%)
  blocking collectives  74.4 us (25%)
  waiting for transfers between devices  58.1 us (20%)
  between operations  14 us (5%)
  matrix products  9.03 us (3%)
  local copies, waits for them, and re-layouts  7.86 us (3%)
    reduce_sum x28, other arithmetic, one_point(): imag_sum = imag_sum + jnp.sum(factor * jnp.cos(phase_angle), axis=0)  125 us
    psum x1, waiting for transfers between devices, broadcast(): return lax.psum(block, axis)  48.7 us
    psum x2, blocking collectives, broadcast(): return lax.psum(block, axis)  36.6 us
    all_gather x1, blocking collectives, per_device(): lax.all_gather(lower_inv, 'prow', axis=2, tiled=True)  15 us
    all_gather x1, blocking collectives, per_device(): lax.all_gather(upper_inv, 'prow', axis=2, tiled=True)  14.7 us
    ppermute x3, waiting for transfers between devices, per_device(): lax.ppermute(incoming, 'prow', [(dev, dev ^ hop) for dev in range(8)])  9.35 us
    dot_general x19, matrix products, exact_dot(): return jnp.dot(first_matrix, second_matrix, precision=lax.Precision.HIGHEST)  9.03 us
    all_gather x1, blocking collectives, per_device(): row_block = lax.all_gather(tri_corners, 'pcol', axis=1, tiled=True)  8.18 us
  transfers between devices with their start and end apart: 5, of which 3 were waited for; matrix products, arithmetic and copies ran while one was open for 1% of the time, Pallas kernels for 0%

profile of v1, /device:TPU:0, one launch (start us, length us, event | category | flops | bytes accessed | tf_op | source)
XLA Modules:
  0.0 293.8 jit_solution(9061642003945568666)
XLA Ops:
  7.9 10.7 %psum.21 = s32[4,256]{1,0:T(4,128)S(1)} all-reduce(s32[4,256]{1,0:T(4,128)S(1)} %add_select_fusion), channel_id=1, replica_groups=mesh['prow'=8,'pcol'=4] {'prow'}, use_global_device_ids=true, to_apply=%region_6.8 | all-reduce | flops 1024 | bytes 8192 | tf_op jit(solution)/shard_map/psum | solution.py:34
  19.3 8.2 %all-gather = f32[4,64,9]{1,2,0:T(8,128)S(1)} all-gather(f32[1,64,9]{1,2,0:T(8,128)S(1)} %bitcast.272), channel_id=1, replica_groups=mesh['prow'=8,'pcol'=4] {'pcol'}, dimensions={0}, use_global_device_ids=true | all-gather | bytes 11520 | tf_op jit(solution)/shard_map/all_gather | solution.py:146
  27.9 25.9 %psum.22 = f32[9,256]{1,0:T(8,128)S(1)} all-reduce(f32[9,256]{1,0:T(8,128)S(1)} %select_bitcast_fusion), channel_id=1, replica_groups=mesh['prow'=8,'pcol'=4] {'prow'}, use_global_device_ids=true, to_apply=%region_5.7 | all-reduce | flops 2304 | bytes 18432 | tf_op jit(solution)/shard_map/psum | solution.py:34
  56.0 128.6 %while.18 = (s32[]{:T(128)}, f32[256,128]{1,0:T(8,128)S(1)}, f32[256,128]{1,0:T(8,128)S(1)}, f32[3,7,256]{2,1,0:T(8,128)S(1)}, f32[3,7,128]{2,1,0:T(8,128)S(1)},...) while((s32[]{:T(128)}, f32[256,128]{1,0:T(8,128)S(1)}, ...), condition=%wide.region_25.28_spmd.clone.clone.clone, body=%wide.region_16.27_spmd.clone.clone.clone.sunk | while | flops 23267076 | bytes 3925331 | solution.py:130
  56.4 4.5 %multiply_reduce_fusion.22 = (f32[256,128]{1,0:T(8,128)S(1)}, f32[256,128]{1,0:T(8,128)S(1)}) fusion(f32[256]{0:T(256)S(1)} %bitcast.245, f32[256]{0:T(256)S(1)} %bitcast.243, f32[256]{0:T(256)S(1)} %bitcast.241, f32[7,128]{1,0:T(8,128)S(1)} %get-tuple-element.877, f32[7,128]{1,0:T(8,128)S(1)} %get-tuple-element.878, ...), kind=kLoop, calls=%fused_computation.2.clone.1 | loop fusion | flops 5668864 | bytes 425472 | tf_op jit(solution)/shard_map/while/body/eval_jaxpr/reduce_sum | solution.py:126
  60.8 4.5 %multiply_reduce_fusion.24 = (f32[256,128]{1,0:T(8,128)S(1)}, f32[256,128]{1,0:T(8,128)S(1)}) fusion(f32[7,128]{1,0:T(8,128)S(1)} %get-tuple-element.877, f32[7,128]{1,0:T(8,128)S(1)} %get-tuple-element.878, f32[7,128]{1,0:T(8,128)S(1)} %get-tuple-element.879, f32[256]{0:T(256)S(1)} %bitcast.257, f32[256]{0:T(256)S(1)} %bitcast.255, ...), kind=kLoop, calls=%fused_computation.4.clone.1 | loop fusion | flops 5668864 | bytes 425472 | tf_op jit(solution)/shard_map/while/body/eval_jaxpr/reduce_sum | solution.py:126
  65.3 4.5 %multiply_reduce_fusion.25 = (f32[256,128]{1,0:T(8,128)S(1)}, f32[256,128]{1,0:T(8,128)S(1)}) fusion(f32[7,128]{1,0:T(8,128)S(1)} %get-tuple-element.889, f32[256]{0:T(256)S(1)} %bitcast.258, f32[7,128]{1,0:T(8,128)S(1)} %get-tuple-element.890, f32[256]{0:T(256)S(1)} %bitcast.256, f32[7,128]{1,0:T(8,128)S(1)} %get-tuple-element.891, ...), kind=kLoop, calls=%fused_computation.5.clone.1 | loop fusion | flops 5668864 | bytes 425472 | tf_op jit(solution)/shard_map/while/body/eval_jaxpr/reduce_sum | solution.py:126
  69.8 4.5 %multiply_reduce_fusion.23 = (f32[256,128]{1,0:T(8,128)S(1)}, f32[256,128]{1,0:T(8,128)S(1)}) fusion(f32[256]{0:T(256)S(1)} %bitcast.246, f32[256]{0:T(256)S(1)} %bitcast.244, f32[256]{0:T(256)S(1)} %bitcast.242, f32[7,128]{1,0:T(8,128)S(1)} %get-tuple-element.889, f32[7,128]{1,0:T(8,128)S(1)} %get-tuple-element.890, ...), kind=kLoop, calls=%fused_computation.3.clone.1 | loop fusion | flops 5668864 | bytes 425472 | tf_op jit(solution)/shard_map/while/body/eval_jaxpr/reduce_sum | solution.py:126
  74.7 4.5 %multiply_reduce_fusion.22 = (f32[256,128]{1,0:T(8,128)S(1)}, f32[256,128]{1,0:T(8,128)S(1)}) fusion(f32[256]{0:T(256)S(1)} %bitcast.245, f32[256]{0:T(256)S(1)} %bitcast.243, f32[256]{0:T(256)S(1)} %bitcast.241, f32[7,128]{1,0:T(8,128)S(1)} %get-tuple-element.877, f32[7,128]{1,0:T(8,128)S(1)} %get-tuple-element.878, ...), kind=kLoop, calls=%fused_computation.2.clone.1 | loop fusion | flops 5668864 | bytes 425472 | tf_op jit(solution)/shard_map/while/body/eval_jaxpr/reduce_sum | solution.py:126
  79.2 4.5 %multiply_reduce_fusion.24 = (f32[256,128]{1,0:T(8,128)S(1)}, f32[256,128]{1,0:T(8,128)S(1)}) fusion(f32[7,128]{1,0:T(8,128)S(1)} %get-tuple-element.877, f32[7,128]{1,0:T(8,128)S(1)} %get-tuple-element.878, f32[7,128]{1,0:T(8,128)S(1)} %get-tuple-element.879, f32[256]{0:T(256)S(1)} %bitcast.257, f32[256]{0:T(256)S(1)} %bitcast.255, ...), kind=kLoop, calls=%fused_computation.4.clone.1 | loop fusion | flops 5668864 | bytes 425472 | tf_op jit(solution)/shard_map/while/body/eval_jaxpr/reduce_sum | solution.py:126
  83.7 4.5 %multiply_reduce_fusion.25 = (f32[256,128]{1,0:T(8,128)S(1)}, f32[256,128]{1,0:T(8,128)S(1)}) fusion(f32[7,128]{1,0:T(8,128)S(1)} %get-tuple-element.889, f32[256]{0:T(256)S(1)} %bitcast.258, f32[7,128]{1,0:T(8,128)S(1)} %get-tuple-element.890, f32[256]{0:T(256)S(1)} %bitcast.256, f32[7,128]{1,0:T(8,128)S(1)} %get-tuple-element.891, ...), kind=kLoop, calls=%fused_computation.5.clone.1 | loop fusion | flops 5668864 | bytes 425472 | tf_op jit(solution)/shard_map/while/body/eval_jaxpr/reduce_sum | solution.py:126
  88.1 4.5 %multiply_reduce_fusion.23 = (f32[256,128]{1,0:T(8,128)S(1)}, f32[256,128]{1,0:T(8,128)S(1)}) fusion(f32[256]{0:T(256)S(1)} %bitcast.246, f32[256]{0:T(256)S(1)} %bitcast.244, f32[256]{0:T(256)S(1)} %bitcast.242, f32[7,128]{1,0:T(8,128)S(1)} %get-tuple-element.889, f32[7,128]{1,0:T(8,128)S(1)} %get-tuple-element.890, ...), kind=kLoop, calls=%fused_computation.3.clone.1 | loop fusion | flops 5668864 | bytes 425472 | tf_op jit(solution)/shard_map/while/body/eval_jaxpr/reduce_sum | solution.py:126
  93.1 4.5 %multiply_reduce_fusion.22 = (f32[256,128]{1,0:T(8,128)S(1)}, f32[256,128]{1,0:T(8,128)S(1)}) fusion(f32[256]{0:T(256)S(1)} %bitcast.245, f32[256]{0:T(256)S(1)} %bitcast.243, f32[256]{0:T(256)S(1)} %bitcast.241, f32[7,128]{1,0:T(8,128)S(1)} %get-tuple-element.877, f32[7,128]{1,0:T(8,128)S(1)} %get-tuple-element.878, ...), kind=kLoop, calls=%fused_computation.2.clone.1 | loop fusion | flops 5668864 | bytes 425472 | tf_op jit(solution)/shard_map/while/body/eval_jaxpr/reduce_sum | solution.py:126
  97.6 4.5 %multiply_reduce_fusion.24 = (f32[256,128]{1,0:T(8,128)S(1)}, f32[256,128]{1,0:T(8,128)S(1)}) fusion(f32[7,128]{1,0:T(8,128)S(1)} %get-tuple-element.877, f32[7,128]{1,0:T(8,128)S(1)} %get-tuple-element.878, f32[7,128]{1,0:T(8,128)S(1)} %get-tuple-element.879, f32[256]{0:T(256)S(1)} %bitcast.257, f32[256]{0:T(256)S(1)} %bitcast.255, ...), kind=kLoop, calls=%fused_computation.4.clone.1 | loop fusion | flops 5668864 | bytes 425472 | tf_op jit(solution)/shard_map/while/body/eval_jaxpr/reduce_sum | solution.py:126
  102.0 4.5 %multiply_reduce_fusion.25 = (f32[256,128]{1,0:T(8,128)S(1)}, f32[256,128]{1,0:T(8,128)S(1)}) fusion(f32[7,128]{1,0:T(8,128)S(1)} %get-tuple-element.889, f32[256]{0:T(256)S(1)} %bitcast.258, f32[7,128]{1,0:T(8,128)S(1)} %get-tuple-element.890, f32[256]{0:T(256)S(1)} %bitcast.256, f32[7,128]{1,0:T(8,128)S(1)} %get-tuple-element.891, ...), kind=kLoop, calls=%fused_computation.5.clone.1 | loop fusion | flops 5668864 | bytes 425472 | tf_op jit(solution)/shard_map/while/body/eval_jaxpr/reduce_sum | solution.py:126
  106.5 4.5 %multiply_reduce_fusion.23 = (f32[256,128]{1,0:T(8,128)S(1)}, f32[256,128]{1,0:T(8,128)S(1)}) fusion(f32[256]{0:T(256)S(1)} %bitcast.246, f32[256]{0:T(256)S(1)} %bitcast.244, f32[256]{0:T(256)S(1)} %bitcast.242, f32[7,128]{1,0:T(8,128)S(1)} %get-tuple-element.889, f32[7,128]{1,0:T(8,128)S(1)} %get-tuple-element.890, ...), kind=kLoop, calls=%fused_computation.3.clone.1 | loop fusion | flops 5668864 | bytes 425472 | tf_op jit(solution)/shard_map/while/body/eval_jaxpr/reduce_sum | solution.py:126
  111.5 4.5 %multiply_reduce_fusion.22 = (f32[256,128]{1,0:T(8,128)S(1)}, f32[256,128]{1,0:T(8,128)S(1)}) fusion(f32[256]{0:T(256)S(1)} %bitcast.245, f32[256]{0:T(256)S(1)} %bitcast.243, f32[256]{0:T(256)S(1)} %bitcast.241, f32[7,128]{1,0:T(8,128)S(1)} %get-tuple-element.877, f32[7,128]{1,0:T(8,128)S(1)} %get-tuple-element.878, ...), kind=kLoop, calls=%fused_computation.2.clone.1 | loop fusion | flops 5668864 | bytes 425472 | tf_op jit(solution)/shard_map/while/body/eval_jaxpr/reduce_sum | solution.py:126
  115.9 4.5 %multiply_reduce_fusion.24 = (f32[256,128]{1,0:T(8,128)S(1)}, f32[256,128]{1,0:T(8,128)S(1)}) fusion(f32[7,128]{1,0:T(8,128)S(1)} %get-tuple-element.877, f32[7,128]{1,0:T(8,128)S(1)} %get-tuple-element.878, f32[7,128]{1,0:T(8,128)S(1)} %get-tuple-element.879, f32[256]{0:T(256)S(1)} %bitcast.257, f32[256]{0:T(256)S(1)} %bitcast.255, ...), kind=kLoop, calls=%fused_computation.4.clone.1 | loop fusion | flops 5668864 | bytes 425472 | tf_op jit(solution)/shard_map/while/body/eval_jaxpr/reduce_sum | solution.py:126
  120.4 4.5 %multiply_reduce_fusion.25 = (f32[256,128]{1,0:T(8,128)S(1)}, f32[256,128]{1,0:T(8,128)S(1)}) fusion(f32[7,128]{1,0:T(8,128)S(1)} %get-tuple-element.889, f32[256]{0:T(256)S(1)} %bitcast.258, f32[7,128]{1,0:T(8,128)S(1)} %get-tuple-element.890, f32[256]{0:T(256)S(1)} %bitcast.256, f32[7,128]{1,0:T(8,128)S(1)} %get-tuple-element.891, ...), kind=kLoop, calls=%fused_computation.5.clone.1 | loop fusion | flops 5668864 | bytes 425472 | tf_op jit(solution)/shard_map/while/body/eval_jaxpr/reduce_sum | solution.py:126
  124.9 4.5 %multiply_reduce_fusion.23 = (f32[256,128]{1,0:T(8,128)S(1)}, f32[256,128]{1,0:T(8,128)S(1)}) fusion(f32[256]{0:T(256)S(1)} %bitcast.246, f32[256]{0:T(256)S(1)} %bitcast.244, f32[256]{0:T(256)S(1)} %bitcast.242, f32[7,128]{1,0:T(8,128)S(1)} %get-tuple-element.889, f32[7,128]{1,0:T(8,128)S(1)} %get-tuple-element.890, ...), kind=kLoop, calls=%fused_computation.3.clone.1 | loop fusion | flops 5668864 | bytes 425472 | tf_op jit(solution)/shard_map/while/body/eval_jaxpr/reduce_sum | solution.py:126
  129.9 4.5 %multiply_reduce_fusion.22 = (f32[256,128]{1,0:T(8,128)S(1)}, f32[256,128]{1,0:T(8,128)S(1)}) fusion(f32[256]{0:T(256)S(1)} %bitcast.245, f32[256]{0:T(256)S(1)} %bitcast.243, f32[256]{0:T(256)S(1)} %bitcast.241, f32[7,128]{1,0:T(8,128)S(1)} %get-tuple-element.877, f32[7,128]{1,0:T(8,128)S(1)} %get-tuple-element.878, ...), kind=kLoop, calls=%fused_computation.2.clone.1 | loop fusion | flops 5668864 | bytes 425472 | tf_op jit(solution)/shard_map/while/body/eval_jaxpr/reduce_sum | solution.py:126
  134.3 4.5 %multiply_reduce_fusion.24 = (f32[256,128]{1,0:T(8,128)S(1)}, f32[256,128]{1,0:T(8,128)S(1)}) fusion(f32[7,128]{1,0:T(8,128)S(1)} %get-tuple-element.877, f32[7,128]{1,0:T(8,128)S(1)} %get-tuple-element.878, f32[7,128]{1,0:T(8,128)S(1)} %get-tuple-element.879, f32[256]{0:T(256)S(1)} %bitcast.257, f32[256]{0:T(256)S(1)} %bitcast.255, ...), kind=kLoop, calls=%fused_computation.4.clone.1 | loop fusion | flops 5668864 | bytes 425472 | tf_op jit(solution)/shard_map/while/body/eval_jaxpr/reduce_sum | solution.py:126
  138.8 4.5 %multiply_reduce_fusion.25 = (f32[256,128]{1,0:T(8,128)S(1)}, f32[256,128]{1,0:T(8,128)S(1)}) fusion(f32[7,128]{1,0:T(8,128)S(1)} %get-tuple-element.889, f32[256]{0:T(256)S(1)} %bitcast.258, f32[7,128]{1,0:T(8,128)S(1)} %get-tuple-element.890, f32[256]{0:T(256)S(1)} %bitcast.256, f32[7,128]{1,0:T(8,128)S(1)} %get-tuple-element.891, ...), kind=kLoop, calls=%fused_computation.5.clone.1 | loop fusion | flops 5668864 | bytes 425472 | tf_op jit(solution)/shard_map/while/body/eval_jaxpr/reduce_sum | solution.py:126
  143.2 4.5 %multiply_reduce_fusion.23 = (f32[256,128]{1,0:T(8,128)S(1)}, f32[256,128]{1,0:T(8,128)S(1)}) fusion(f32[256]{0:T(256)S(1)} %bitcast.246, f32[256]{0:T(256)S(1)} %bitcast.244, f32[256]{0:T(256)S(1)} %bitcast.242, f32[7,128]{1,0:T(8,128)S(1)} %get-tuple-element.889, f32[7,128]{1,0:T(8,128)S(1)} %get-tuple-element.890, ...), kind=kLoop, calls=%fused_computation.3.clone.1 | loop fusion | flops 5668864 | bytes 425472 | tf_op jit(solution)/shard_map/while/body/eval_jaxpr/reduce_sum | solution.py:126
  148.2 4.5 %multiply_reduce_fusion.22 = (f32[256,128]{1,0:T(8,128)S(1)}, f32[256,128]{1,0:T(8,128)S(1)}) fusion(f32[256]{0:T(256)S(1)} %bitcast.245, f32[256]{0:T(256)S(1)} %bitcast.243, f32[256]{0:T(256)S(1)} %bitcast.241, f32[7,128]{1,0:T(8,128)S(1)} %get-tuple-element.877, f32[7,128]{1,0:T(8,128)S(1)} %get-tuple-element.878, ...), kind=kLoop, calls=%fused_computation.2.clone.1 | loop fusion | flops 5668864 | bytes 425472 | tf_op jit(solution)/shard_map/while/body/eval_jaxpr/reduce_sum | solution.py:126
  152.7 4.5 %multiply_reduce_fusion.24 = (f32[256,128]{1,0:T(8,128)S(1)}, f32[256,128]{1,0:T(8,128)S(1)}) fusion(f32[7,128]{1,0:T(8,128)S(1)} %get-tuple-element.877, f32[7,128]{1,0:T(8,128)S(1)} %get-tuple-element.878, f32[7,128]{1,0:T(8,128)S(1)} %get-tuple-element.879, f32[256]{0:T(256)S(1)} %bitcast.257, f32[256]{0:T(256)S(1)} %bitcast.255, ...), kind=kLoop, calls=%fused_computation.4.clone.1 | loop fusion | flops 5668864 | bytes 425472 | tf_op jit(solution)/shard_map/while/body/eval_jaxpr/reduce_sum | solution.py:126
  157.2 4.5 %multiply_reduce_fusion.25 = (f32[256,128]{1,0:T(8,128)S(1)}, f32[256,128]{1,0:T(8,128)S(1)}) fusion(f32[7,128]{1,0:T(8,128)S(1)} %get-tuple-element.889, f32[256]{0:T(256)S(1)} %bitcast.258, f32[7,128]{1,0:T(8,128)S(1)} %get-tuple-element.890, f32[256]{0:T(256)S(1)} %bitcast.256, f32[7,128]{1,0:T(8,128)S(1)} %get-tuple-element.891, ...), kind=kLoop, calls=%fused_computation.5.clone.1 | loop fusion | flops 5668864 | bytes 425472 | tf_op jit(solution)/shard_map/while/body/eval_jaxpr/reduce_sum | solution.py:126
  161.6 4.5 %multiply_reduce_fusion.23 = (f32[256,128]{1,0:T(8,128)S(1)}, f32[256,128]{1,0:T(8,128)S(1)}) fusion(f32[256]{0:T(256)S(1)} %bitcast.246, f32[256]{0:T(256)S(1)} %bitcast.244, f32[256]{0:T(256)S(1)} %bitcast.242, f32[7,128]{1,0:T(8,128)S(1)} %get-tuple-element.889, f32[7,128]{1,0:T(8,128)S(1)} %get-tuple-element.890, ...), kind=kLoop, calls=%fused_computation.3.clone.1 | loop fusion | flops 5668864 | bytes 425472 | tf_op jit(solution)/shard_map/while/body/eval_jaxpr/reduce_sum | solution.py:126
  187.8 8.8 %collective-permute-done.1 = f32[256,256]{1,0:T(8,128)S(1)} collective-permute-done((f32[256,256]{1,0:T(8,128)S(1)}, f32[256,256]{1,0:T(8,128)S(1)}, u32[]{:S(2)}, u32[]{:S(2)}) %collective-permute-start.1) | collective-permute-done | bytes 262176 | tf_op jit(solution)/shard_map/ppermute | solution.py:182
  196.7 48.7 %all-reduce.3.cloned.1.call-done = f32[256,256]{0,1:T(8,128)} async-done(((f32[256,256]{0,1:T(8,128)}), f32[256,256]{0,1:T(8,128)}) %all-reduce.3.cloned.1.call-update) | async-done | bytes 262160 | tf_op jit(solution)/shard_map/psum | solution.py:34
  248.8 15.0 %all_gather.15 = f32[1,2,256,256]{3,2,1,0:T(8,128)S(1)} all-gather(f32[1,2,32,256]{3,2,1,0:T(8,128)S(1)} %copy-done.1), channel_id=1, replica_groups=mesh['prow'=8,'pcol'=4] {'prow'}, dimensions={2}, use_global_device_ids=true | all-gather | bytes 589824 | tf_op jit(solution)/shard_map/all_gather | solution.py:167
  263.7 14.7 %all_gather.14 = f32[1,2,256,256]{3,2,1,0:T(8,128)S(1)} all-gather(f32[1,2,32,256]{3,2,1,0:T(8,128)S(1)} %copy-done.2), channel_id=1, replica_groups=mesh['prow'=8,'pcol'=4] {'prow'}, dimensions={2}, use_global_device_ids=true | all-gather | bytes 589824 | tf_op jit(solution)/shard_map/all_gather | solution.py:168
  (239 shorter events, 40.1 us)
Async XLA Ops:
  6.5 238.8 %all-reduce.3.cloned.1.call-start = ((), (), s32[]{:S(2)}) async-start(), calls=%async_computation | async-start | bytes 524288 | tf_op jit(solution)/shard_map/psum | solution.py:34
  6.5 0.7 copy-start.6
  7.2 0.7 copy-start.7
  18.6 0.7 copy-start.5
  55.3 0.7 copy-start.3
  184.8 0.7 copy-start.4
  185.8 1.6 collective-permute-start
  186.7 93.4 %all-gather.3.cloned.1.call-start = ((), (), s32[]{:S(2)}) async-start(), calls=%async_computation.1 | async-start | bytes 1310720 | tf_op jit(solution)/shard_map/all_gather | solution.py:199
  187.5 9.1 %collective-permute-start.1 = (f32[256,256]{1,0:T(8,128)S(1)}, f32[256,256]{1,0:T(8,128)S(1)}, u32[]{:S(2)}, u32[]{:S(2)}) collective-permute-start(f32[256,256]{1,0:T(8,128)S(1)} %add.524), channel_id=1, source_target_pairs={{0,8},{4,12},{8,0},{12,4},{16,24},{20,28},{24,16},{28,20},{1,9},{5... | collective-permute-start | bytes 786440 | tf_op jit(solution)/shard_map/ppermute | solution.py:182
  196.6 50.1 %collective-permute-start.2 = (f32[256,256]{1,0:T(8,128)S(1)}, f32[256,256]{1,0:T(8,128)S(1)}, u32[]{:S(2)}, u32[]{:S(2)}) collective-permute-start(f32[256,256]{1,0:T(8,128)S(1)} %add.525), channel_id=1, source_target_pairs={{0,16},{4,20},{8,24},{12,28},{16,0},{20,4},{24,8},{28,12},{1,17},{... | collective-permute-start | bytes 786440 | tf_op jit(solution)/shard_map/ppermute | solution.py:182
  247.9 0.8 copy-start.1
  248.8 15.0 %copy-start.2 = (f32[1,2,32,256]{3,2,1,0:T(8,128)S(1)}, f32[1,2,32,256]{3,2,1,0:T(8,128)}, u32[]{:S(2)}) copy-start(f32[1,2,32,256]{3,2,1,0:T(8,128)} %param.19) | copy-start | bytes 196612
  284.5 1.0 copy-start
Sparse Core Ops, SparseCore 0:
  186.8 58.5 all-reduce.2
  248.1 25.5 all-gather.2
